TPU v7x, 32 devices: a whole 2x2x4 slice. The times are simulated.
32 devices in a mesh: dom: 8 (over z, x), rep: 4 (over y, core).
Axes of the slice: x: 2, y: 2, z: 4, core: 2. Of those that a mesh axis runs over, the one named last changes fastest.
Arguments:
- features: bfloat16 [65536, 128], P('dom'), may hold values from -6 to 6
- weight: bfloat16 [128, 256], replicated, may hold values from -0.5 to 0.5
- out_grad: bfloat16 [65536, 256], P(('dom', 'rep')), may hold values from -6 to 6
- send_rows: int32 [8, 8, 64], P('dom'), may hold values from 0 to 8191, as said below
- send_count: int32 [8, 8], P('dom'), may hold values from 0 to 64, as said below
- tile_target: int32 [8, 4, 256], P('dom', 'rep'), may hold values from 0 to 15, as said below
- tile_source: int32 [8, 4, 256], P('dom', 'rep'), may hold values from 0 to 67, as said below
- tile_weights: bfloat16 [8, 4, 256, 128, 128], P('dom', 'rep'), may hold values from -0.125 to 0.125
Outputs:
- activated: bfloat16 [65536, 256], P(('dom', 'rep'))
- feature_grad: bfloat16 [65536, 128], P(('dom', 'rep'))
- weight_grad: float32 [128, 256], replicated
Inputs may be any that keep to these rules, and one draw needn't show every extreme that they name: Within one list send_rows[o, d] the rows are distinct and increasing; entries at slots c >= send_count[o, d] are ignored. send_count[o, o] is 0. Every owner sends exactly 64 rows to some partition, and every partition receives exactly 64 rows from some owner. `tile_target`: pairs of target and source tiles may repeat. `tile_source`: every halo source tile (64 to 67) is named by some tile of every group.
All inputs are finite; a program needn't handle non-finite values.
Results may differ from a plain program's by a relative error of at most 0.006.
Values may be sent and summed in bfloat16 or wider, within the bound.
No kernel may reach another device: no remote copies, remote signals or barrier semaphores. Data moves between devices by JAX's collectives and lax.ppermute only.
A program may use at most 128 MiB of HBM per device.

v0:
```python
import jax
import jax.numpy as jnp
from jax import lax
from jax.sharding import PartitionSpec as P


def shards(
    features, weight, out_grad, send_rows, send_count, tile_target, tile_source, tile_weights
):
    feat = features.shape[1]
    tile = tile_weights.shape[-1]
    rows = send_rows[0]
    counts = send_count[0]
    width = rows.shape[1]
    valid = jnp.arange(width, dtype=jnp.int32)[None, :] < counts[:, None]
    outgoing = jnp.where(valid[:, :, None], features[rows], jnp.zeros((), jnp.bfloat16))
    halo = lax.all_to_all(outgoing, "dom", split_axis=0, concat_axis=0, tiled=True)
    sources = jnp.concatenate([features, halo.reshape(-1, feat)], axis=0)
    targets = tile_target[0, 0]
    anchors = tile_source[0, 0]
    values = tile_weights[0, 0]
    tgt_count = out_grad.shape[0] // tile
    src_count = sources.shape[0] // tile
    blocks = sources.reshape(src_count, tile, feat)[anchors]
    prods = jnp.einsum("tij,tjf->tif", values, blocks, preferred_element_type=jnp.float32)
    gathered = jax.ops.segment_sum(prods, targets, num_segments=tgt_count)
    gathered = gathered.reshape(-1, feat).astype(jnp.bfloat16)
    pre = jnp.dot(gathered, weight, preferred_element_type=jnp.float32)
    activated = jax.nn.silu(pre).astype(jnp.bfloat16)
    sigma = jax.nn.sigmoid(pre)
    slope = sigma * (1.0 + pre * (1.0 - sigma))
    pre_grad = (out_grad.astype(jnp.float32) * slope).astype(jnp.bfloat16)
    weight_part = jnp.dot(gathered.T, pre_grad, preferred_element_type=jnp.float32)
    weight_grad = lax.psum(weight_part, ("dom", "rep"))
    agg_grad = jnp.dot(pre_grad, weight.T, preferred_element_type=jnp.float32).astype(jnp.bfloat16)
    dblocks = agg_grad.reshape(tgt_count, tile, feat)[targets]
    backward = jnp.einsum("tij,tif->tjf", values, dblocks, preferred_element_type=jnp.float32)
    source_grad = jax.ops.segment_sum(backward, anchors, num_segments=src_count).reshape(-1, feat)
    owned_rows = features.shape[0]
    local = source_grad[:owned_rows]
    incoming = source_grad[owned_rows:].reshape(-1, width, feat)
    returned = lax.all_to_all(incoming, "dom", split_axis=0, concat_axis=0, tiled=True)
    kept = jnp.where(valid[:, :, None], returned, jnp.zeros((), jnp.float32))
    local = local.at[rows.reshape(-1)].add(kept.reshape(-1, feat))
    node_grad = lax.psum_scatter(local, "rep", scatter_dimension=0, tiled=True).astype(jnp.bfloat16)
    return (activated, node_grad, weight_grad)


def solution(mesh):
    return jax.shard_map(
        shards,
        mesh=mesh,
        in_specs=(
            P("dom", None),
            P(),
            P(("dom", "rep"), None),
            P("dom", None, None),
            P("dom", None),
            P("dom", "rep", None),
            P("dom", "rep", None),
            P("dom", "rep", None, None, None),
        ),
        out_specs=(P(("dom", "rep"), None), P(("dom", "rep"), None), P()),
        check_vma=False,
    )
```

profile of v0, /device:TPU:0, one launch (start us, length us, event | category | flops | bytes accessed | tf_op | source)
XLA Modules:
  0.0 379.2 jit_solution(14296807344320537851)
XLA Ops:
  8.0 0.0 copy-start
  8.0 0.8 iota_compare_fusion
  8.8 0.7 compare_select_fusion.1
  9.5 0.1 reshape.170
  9.6 2.9 gather_fusion
  12.5 0.8 broadcast_select_fusion.1
  13.3 7.3 %all-to-all-start = ((bf16[8,64,128]{2,1,0:T(8,128)(2,1)}), bf16[8,64,128]{2,1,0:T(8,128)(2,1)S(1)}, u32[]{:S(2)}, u32[]{:S(2)}) async-start(bf16[8,64,128]{2,1,0:T(8,128)(2,1)} %broadcast_select_fusion.1), calls=%async_computation | async-start | bytes 262144 | tf_op jit(solution)/shard_map/all_to_all | solution.py:17
  20.5 0.7 compare_select_fusion.3
  21.2 0.7 compare_select_fusion.2
  21.9 6.0 %all-to-all-done = bf16[8,64,128]{2,1,0:T(8,128)(2,1)S(1)} async-done(((bf16[8,64,128]{2,1,0:T(8,128)(2,1)}), bf16[8,64,128]{2,1,0:T(8,128)(2,1)S(1)}, u32[]{:S(2)}, u32[]{:S(2)}) %all-to-all-start) | async-done | bytes 131104 | tf_op jit(solution)/shard_map/all_to_all | solution.py:17
  27.9 5.3 %pad_maximum_fusion = bf16[8704,128]{1,0:T(8,128)(2,1)S(1)} fusion(bf16[512,128]{1,0:T(8,128)(2,1)S(1)} %bitcast.45, bf16[8192,128]{1,0:T(8,128)(2,1)} %param.8), kind=kLoop, calls=%fused_computation.11 | loop fusion | flops 4456448 | bytes 4456448 | tf_op jit(solution)/shard_map/concatenate | solution.py:18
  33.2 8.6 %gather_fusion.1 = bf16[256,128,128]{2,1,0:T(8,128)(2,1)} fusion(bf16[68,128,128]{2,1,0:T(8,128)(2,1)S(1)} %bitcast.40, s32[1024]{0:T(1024)S(1)} %pad_clamp_fusion.1), kind=kCustom, calls=%fused_computation.1 | custom fusion | bytes 16778240 | tf_op jit(solution)/shard_map/gather | solution.py:24
  41.9 12.8 %convolution_bitcast_fusion.1 = f32[256,128,128]{1,2,0:T(8,128)} fusion(bf16[256,128,128]{2,1,0:T(8,128)(2,1)} %gather_fusion.1, bf16[1,1,256,128,128]{4,3,2,1,0:T(8,128)(2,1)} %param.15), kind=kOutput, calls=%fused_computation.7 | convolution fusion | flops 1073741824 | bytes 33554432 | tf_op jit(solution)/shard_map/tij,tjf->tif/dot_general | solution.py:25
  54.7 0.0 copy-start.3
  54.7 17.5 %copy.14 = f32[256,128,128]{2,1,0:T(8,128)} copy(f32[256,128,128]{1,2,0:T(8,128)} %convolution_bitcast_fusion.1) | data formatting | bytes 33554432 | tf_op jit(solution)/shard_map/tij,tjf->tif/dot_general | solution.py:25
  72.2 0.1 broadcast_in_dim.35
  72.3 0.0 copy-done.3
  72.3 0.0 copy-start.5
  72.3 33.2 %scatter_fusion = f32[16,128,128]{2,1,0:T(8,128)S(1)} fusion(f32[16,128,128]{2,1,0:T(8,128)S(1)} %broadcast_in_dim.35, s32[256]{0:T(256)S(1)} %bitcast.48, f32[256,128,128]{2,1,0:T(8,128)} %copy.14), kind=kCustom, calls=%fused_computation.3 | custom fusion | flops 4194304 | bytes 50332672 | tf_op jit(solution)/shard_map/scatter-add | solution.py:26
  105.5 0.1 convert_element_type.21
  105.6 0.0 copy-done
  105.6 0.0 copy-done.5
  105.6 2.1 multiply_convert_fusion
  107.7 0.4 convolution_convert_fusion
  108.1 8.8 %gather_fusion.2 = bf16[256,128,128]{2,1,0:T(8,128)(2,1)} fusion(bf16[16,128,128]{2,1,0:T(8,128)(2,1)S(1)} %bitcast.39, s32[1024]{0:T(1024)S(1)} %pad_clamp_fusion), kind=kCustom, calls=%fused_computation.2 | custom fusion | bytes 16778240 | tf_op jit(solution)/shard_map/gather | solution.py:36
  116.9 14.4 %convolution_bitcast_fusion = f32[256,128,128]{1,2,0:T(8,128)} fusion(bf16[256,128,128]{2,1,0:T(8,128)(2,1)} %gather_fusion.2, bf16[1,1,256,128,128]{4,3,2,1,0:T(8,128)(2,1)} %param.15), kind=kOutput, calls=%fused_computation.6 | convolution fusion | flops 1073741824 | bytes 33554432 | tf_op jit(solution)/shard_map/tij,tif->tjf/dot_general | solution.py:37
  131.3 0.0 copy-start.4
  131.3 17.5 %copy.16 = f32[256,128,128]{2,1,0:T(8,128)} copy(f32[256,128,128]{1,2,0:T(8,128)} %convolution_bitcast_fusion) | data formatting | bytes 33554432 | tf_op jit(solution)/shard_map/tij,tif->tjf/dot_general | solution.py:37
  148.8 2.6 broadcast_in_dim.38
  151.3 0.0 copy-done.4
  151.3 0.0 copy-start.2
  151.3 51.9 %scatter_fusion.1 = f32[68,128,128]{2,1,0:T(8,128)} fusion(f32[68,128,128]{2,1,0:T(8,128)} %broadcast_in_dim.38, s32[256]{0:T(256)S(1)} %bitcast.49, f32[256,128,128]{2,1,0:T(8,128)} %copy.16), kind=kCustom, calls=%fused_computation.4 | custom fusion | flops 4194304 | bytes 50332672 | tf_op jit(solution)/shard_map/scatter-add | solution.py:38
  203.2 1.7 slice.20
  204.9 3.4 all-to-all-start.1
  208.3 0.0 reduce-scatter.2.cloned.1.call-start
  208.3 0.0 copy-done.2
  208.4 0.1 reshape_squeeze.3
  208.4 0.0 copy-start.1
  208.4 4.7 %slice.19 = f32[64,128,128]{2,1,0:T(8,128)} slice(f32[68,128,128]{2,1,0:T(8,128)} %scatter_fusion.1), slice={[0:64], [0:128], [0:128]} | slice | bytes 8388608 | tf_op jit(solution)/shard_map/slice | solution.py:40
  213.1 3.4 all-to-all-done.1
  216.5 0.1 broadcast_select_fusion
  216.6 7.1 %scatter_fusion.2 = f32[8192,128]{1,0:T(8,128)} fusion(f32[8192,128]{1,0:T(8,128)} %bitcast.41, s32[512]{0:T(512)S(1)} %bitcast.47, f32[512,128]{1,0:T(8,128)S(1)} %bitcast.44), kind=kCustom, calls=%fused_computation.5 | custom fusion | flops 65536 | bytes 788480 | tf_op jit(solution)/shard_map/scatter-add | solution.py:44
  223.8 0.0 reduce-scatter.2.cloned.1.call-update
  223.8 0.0 all-reduce.2.cloned.1.call-start
  223.8 1.0 fusion.2
  224.8 0.0 all-reduce.2.cloned.1.call-update
  224.9 42.1 %reduce-scatter.2.cloned.1.call-done = f32[2048,128]{1,0:T(8,128)} async-done(((f32[8192,128]{1,0:T(8,128)}), f32[2048,128]{1,0:T(8,128)}) %reduce-scatter.2.cloned.1.call-update) | async-done | bytes 1048592 | tf_op jit(solution)/shard_map/reduce_scatter | solution.py:45
  267.0 2.1 convert_element_type.27
  269.1 101.1 %all-reduce.2.cloned.1.call-done = f32[128,256]{1,0:T(8,128)} async-done(((f32[128,256]{1,0:T(8,128)}), f32[128,256]{1,0:T(8,128)}) %all-reduce.2.cloned.1.call-update) | async-done | bytes 131088 | tf_op jit(solution)/shard_map/psum | solution.py:34
  370.2 1.6 copy.23
  371.7 0.0 copy-done.1
  (4 shorter events, 0.0 us)
Async XLA Ops:
  8.0 97.6 %copy-start = (bf16[128,256]{1,0:T(8,128)(2,1)S(1)}, bf16[128,256]{1,0:T(8,128)(2,1)}, u32[]{:S(2)}) copy-start(bf16[128,256]{1,0:T(8,128)(2,1)} %param.9) | copy-start | bytes 196612
  13.3 14.6 %all-to-all-start = ((bf16[8,64,128]{2,1,0:T(8,128)(2,1)}), bf16[8,64,128]{2,1,0:T(8,128)(2,1)S(1)}, u32[]{:S(2)}, u32[]{:S(2)}) async-start(bf16[8,64,128]{2,1,0:T(8,128)(2,1)} %broadcast_select_fusion.1), calls=%async_computation | async-start | bytes 262144 | tf_op jit(solution)/shard_map/all_to_all | solution.py:17
  54.7 17.6 %copy-start.3 = (s32[1,1,256]{2,1,0:T(1,128)S(1)}, s32[1,1,256]{2,1,0:T(1,128)}, u32[]{:S(2)}) copy-start(s32[1,1,256]{2,1,0:T(1,128)} %param.13) | copy-start | bytes 3076
  72.3 33.3 %copy-start.5 = (bf16[2048,256]{1,0:T(8,128)(2,1)S(1)}, bf16[2048,256]{1,0:T(8,128)(2,1)}, u32[]{:S(2)}) copy-start(bf16[2048,256]{1,0:T(8,128)(2,1)} %param.10) | copy-start | bytes 3145732
  131.3 20.0 %copy-start.4 = (s32[1,1,256]{2,1,0:T(1,128)S(1)}, s32[1,1,256]{2,1,0:T(1,128)}, u32[]{:S(2)}) copy-start(s32[1,1,256]{2,1,0:T(1,128)} %param.14) | copy-start | bytes 3076
  151.3 57.0 %copy-start.2 = (s32[1,8,64]{2,1,0:T(8,128)S(1)}, s32[1,8,64]{2,1,0:T(8,128)}, u32[]{:S(2)}) copy-start(s32[1,8,64]{2,1,0:T(8,128)} %param.11) | copy-start | bytes 6148
  204.9 11.6 %all-to-all-start.1 = ((f32[8,64,128]{2,1,0:T(8,128)}), f32[8,64,128]{2,1,0:T(8,128)S(1)}, u32[]{:S(2)}, u32[]{:S(2)}) async-start(f32[8,64,128]{2,1,0:T(8,128)} %bitcast.18), calls=%async_computation.1 | async-start | bytes 524288 | tf_op jit(solution)/shard_map/all_to_all | solution.py:42
  208.3 58.7 %reduce-scatter.2.cloned.1.call-start = ((), (), s32[]{:S(2)}) async-start(), calls=%async_computation.3 | async-start | bytes 5242880 | tf_op jit(solution)/shard_map/reduce_scatter | solution.py:45
  208.4 163.3 %copy-start.1 = (bf16[128,256]{1,0:T(8,128)(2,1)S(1)}, bf16[128,256]{1,0:T(8,128)(2,1)}, u32[]{:S(2)}) copy-start(bf16[128,256]{1,0:T(8,128)(2,1)} %param.9) | copy-start | bytes 196612
  223.8 146.4 %all-reduce.2.cloned.1.call-start = ((), (), s32[]{:S(2)}) async-start(), calls=%async_computation.4 | async-start | bytes 262144 | tf_op jit(solution)/shard_map/psum | solution.py:34
Sparse Core Ops, SparseCore 0:
  223.9 43.0 reduce-scatter.1
Sparse Core Ops, SparseCore 1:
  230.4 139.7 all-reduce.1
where the time goes:
time: 381 us; the launch traced here: 379 us
  waiting for transfers between devices  153 us (40%)
  other arithmetic  103 us (27%)
  local copies, waits for them, and re-layouts  66 us (17%)
  matrix products  30.7 us (8%)
  between operations  15.6 us (4%)
  starting transfers between devices  10.8 us (3%)
    psum x1, waiting for transfers between devices, shards(): weight_grad = lax.psum(weight_part, ('dom', 'rep'))  101 us
    scatter-add x1, other arithmetic, shards(): jax.ops.segment_sum(backward, anchors, num_segments=src_count)  51.9 us
    reduce_scatter x1, waiting for transfers between devices, shards(): lax.psum_scatter(local, 'rep', scatter_dimension=0, tiled=True)  42.1 us
    scatter-add x1, other arithmetic, shards(): gathered = jax.ops.segment_sum(prods, targets, num_segments=tgt_count)  33.2 us
    dot_general x1, local copies, waits for them, and re-layouts, shards(): jnp.einsum('tij,tjf->tif', values, blocks, preferred_element_type=jnp.flo...  17.5 us
    dot_general x1, local copies, waits for them, and re-layouts, shards(): jnp.einsum('tij,tif->tjf', values, dblocks, preferred_element_type=jnp.fl...  17.5 us
    dot_general x1, matrix products, shards(): jnp.einsum('tij,tif->tjf', values, dblocks, preferred_element_type=jnp.fl...  14.4 us
    dot_general x1, matrix products, shards(): jnp.einsum('tij,tjf->tif', values, blocks, preferred_element_type=jnp.flo...  12.8 us
  transfers between devices with their start and end apart: 4, of which 4 were waited for; matrix products, arithmetic and copies ran while one was open for 2% of the time, Pallas kernels for 0%

commit v1 on v0

--- a/solution.py
+++ b/solution.py
@@ -31,7 +31,7 @@
     slope = sigma * (1.0 + pre * (1.0 - sigma))
     pre_grad = (out_grad.astype(jnp.float32) * slope).astype(jnp.bfloat16)
     weight_part = jnp.dot(gathered.T, pre_grad, preferred_element_type=jnp.float32)
-    weight_grad = lax.psum(weight_part, ("dom", "rep"))
+    weight_grad = lax.psum(lax.psum(weight_part, "dom"), "rep")
     agg_grad = jnp.dot(pre_grad, weight.T, preferred_element_type=jnp.float32).astype(jnp.bfloat16)
     dblocks = agg_grad.reshape(tgt_count, tile, feat)[targets]
     backward = jnp.einsum("tij,tif->tjf", values, dblocks, preferred_element_type=jnp.float32)

time: 381 us -> 328 us (0.86)
  waiting for transfers between devices: 153 us -> 98.5 us
    reduce_scatter x1, waiting for transfers between devices: 42.1 us -> 0.03 us  [shards(): lax.psum_scatter(local, 'rep', scatter_dimension=0, tiled=True)]
    psum x1 -> x2, waiting for transfers between devices: 101 us -> 90.9 us  [shards(): weight_grad = lax.psum(lax.psum(weight_part, 'dom'), 'rep')]
  transfers between devices with their start and end apart: 4 -> 5, of which waited for: 4 -> 4; matrix products, arithmetic and copies ran while one was open for 2% -> 5% of each run, Pallas kernels for 0% -> 0%
where the time goes in v1:
time: 328 us; the launch traced here: 325 us
  other arithmetic  103 us (31%)
  waiting for transfers between devices  98.5 us (30%)
  local copies, waits for them, and re-layouts  66.7 us (20%)
  matrix products  30.7 us (9%)
  between operations  15.6 us (5%)
  starting transfers between devices  10.8 us (3%)
    psum x2, waiting for transfers between devices, shards(): weight_grad = lax.psum(lax.psum(weight_part, 'dom'), 'rep')  90.9 us
    scatter-add x1, other arithmetic, shards(): jax.ops.segment_sum(backward, anchors, num_segments=src_count)  51.5 us
    scatter-add x1, other arithmetic, shards(): gathered = jax.ops.segment_sum(prods, targets, num_segments=tgt_count)  33.2 us
    dot_general x1, local copies, waits for them, and re-layouts, shards(): jnp.einsum('tij,tjf->tif', values, blocks, preferred_element_type=jnp.flo...  17.5 us
    dot_general x1, local copies, waits for them, and re-layouts, shards(): jnp.einsum('tij,tif->tjf', values, dblocks, preferred_element_type=jnp.fl...  17.5 us
    dot_general x1, matrix products, shards(): jnp.einsum('tij,tif->tjf', values, dblocks, preferred_element_type=jnp.fl...  14.4 us
    dot_general x1, matrix products, shards(): jnp.einsum('tij,tjf->tif', values, blocks, preferred_element_type=jnp.flo...  12.8 us
    gather x1, local copies, waits for them, and re-layouts, shards(): dblocks = agg_grad.reshape(tgt_count, tile, feat)[targets]  8.77 us
  transfers between devices with their start and end apart: 5, of which 4 were waited for; matrix products, arithmetic and copies ran while one was open for 5% of the time, Pallas kernels for 0%

profile of v1, /device:TPU:0, one launch (start us, length us, event | category | flops | bytes accessed | tf_op | source)
XLA Modules:
  0.0 325.4 jit_solution(9100214656433500407)
XLA Ops:
  8.0 0.0 copy-start
  8.0 0.8 iota_compare_fusion
  8.8 0.7 compare_select_fusion.1
  9.5 0.1 reshape.170
  9.6 2.9 gather_fusion
  12.5 0.8 broadcast_select_fusion.1
  13.3 7.3 %all-to-all-start = ((bf16[8,64,128]{2,1,0:T(8,128)(2,1)}), bf16[8,64,128]{2,1,0:T(8,128)(2,1)S(1)}, u32[]{:S(2)}, u32[]{:S(2)}) async-start(bf16[8,64,128]{2,1,0:T(8,128)(2,1)} %broadcast_select_fusion.1), calls=%async_computation | async-start | bytes 262144 | tf_op jit(solution)/shard_map/all_to_all | solution.py:17
  20.5 0.7 compare_select_fusion.3
  21.2 0.7 compare_select_fusion.2
  21.9 0.8 reshape_squeeze.3
  22.7 5.2 %all-to-all-done = bf16[8,64,128]{2,1,0:T(8,128)(2,1)S(1)} async-done(((bf16[8,64,128]{2,1,0:T(8,128)(2,1)}), bf16[8,64,128]{2,1,0:T(8,128)(2,1)S(1)}, u32[]{:S(2)}, u32[]{:S(2)}) %all-to-all-start) | async-done | bytes 131104 | tf_op jit(solution)/shard_map/all_to_all | solution.py:17
  27.9 5.3 %pad_maximum_fusion = bf16[8704,128]{1,0:T(8,128)(2,1)S(1)} fusion(bf16[512,128]{1,0:T(8,128)(2,1)S(1)} %bitcast.45, bf16[8192,128]{1,0:T(8,128)(2,1)} %param.8), kind=kLoop, calls=%fused_computation.11 | loop fusion | flops 4456448 | bytes 4456448 | tf_op jit(solution)/shard_map/concatenate | solution.py:18
  33.2 8.6 %gather_fusion.1 = bf16[256,128,128]{2,1,0:T(8,128)(2,1)} fusion(bf16[68,128,128]{2,1,0:T(8,128)(2,1)S(1)} %bitcast.40, s32[1024]{0:T(1024)S(1)} %pad_clamp_fusion.1), kind=kCustom, calls=%fused_computation.1 | custom fusion | bytes 16778240 | tf_op jit(solution)/shard_map/gather | solution.py:24
  41.8 12.8 %convolution_bitcast_fusion.1 = f32[256,128,128]{1,2,0:T(8,128)} fusion(bf16[256,128,128]{2,1,0:T(8,128)(2,1)} %gather_fusion.1, bf16[1,1,256,128,128]{4,3,2,1,0:T(8,128)(2,1)} %param.15), kind=kOutput, calls=%fused_computation.7 | convolution fusion | flops 1073741824 | bytes 33554432 | tf_op jit(solution)/shard_map/tij,tjf->tif/dot_general | solution.py:25
  54.7 0.0 copy-start.2
  54.7 17.5 %copy.14 = f32[256,128,128]{2,1,0:T(8,128)} copy(f32[256,128,128]{1,2,0:T(8,128)} %convolution_bitcast_fusion.1) | data formatting | bytes 33554432 | tf_op jit(solution)/shard_map/tij,tjf->tif/dot_general | solution.py:25
  72.2 0.1 broadcast_in_dim.35
  72.3 0.0 copy-done.2
  72.3 0.0 copy-start.4
  72.3 33.2 %scatter_fusion = f32[16,128,128]{2,1,0:T(8,128)S(1)} fusion(f32[16,128,128]{2,1,0:T(8,128)S(1)} %broadcast_in_dim.35, s32[256]{0:T(256)S(1)} %bitcast.48, f32[256,128,128]{2,1,0:T(8,128)} %copy.14), kind=kCustom, calls=%fused_computation.3 | custom fusion | flops 4194304 | bytes 50332672 | tf_op jit(solution)/shard_map/scatter-add | solution.py:26
  105.5 0.1 convert_element_type.21
  105.6 0.0 copy-done
  105.6 0.0 copy-done.4
  105.6 2.1 multiply_convert_fusion
  107.7 0.4 convolution_convert_fusion
  108.1 8.8 %gather_fusion.2 = bf16[256,128,128]{2,1,0:T(8,128)(2,1)} fusion(bf16[16,128,128]{2,1,0:T(8,128)(2,1)S(1)} %bitcast.39, s32[1024]{0:T(1024)S(1)} %pad_clamp_fusion), kind=kCustom, calls=%fused_computation.2 | custom fusion | bytes 16778240 | tf_op jit(solution)/shard_map/gather | solution.py:36
  116.9 14.4 %convolution_bitcast_fusion = f32[256,128,128]{1,2,0:T(8,128)} fusion(bf16[256,128,128]{2,1,0:T(8,128)(2,1)} %gather_fusion.2, bf16[1,1,256,128,128]{4,3,2,1,0:T(8,128)(2,1)} %param.15), kind=kOutput, calls=%fused_computation.6 | convolution fusion | flops 1073741824 | bytes 33554432 | tf_op jit(solution)/shard_map/tij,tif->tjf/dot_general | solution.py:37
  131.2 0.0 copy-start.3
  131.2 17.5 %copy.16 = f32[256,128,128]{2,1,0:T(8,128)} copy(f32[256,128,128]{1,2,0:T(8,128)} %convolution_bitcast_fusion) | data formatting | bytes 33554432 | tf_op jit(solution)/shard_map/tij,tif->tjf/dot_general | solution.py:37
  148.7 2.6 broadcast_in_dim.38
  151.3 0.0 copy-done.3
  151.3 51.5 %scatter_fusion.1 = f32[68,128,128]{2,1,0:T(8,128)} fusion(f32[68,128,128]{2,1,0:T(8,128)} %broadcast_in_dim.38, s32[256]{0:T(256)S(1)} %bitcast.49, f32[256,128,128]{2,1,0:T(8,128)} %copy.16), kind=kCustom, calls=%fused_computation.4 | custom fusion | flops 4194304 | bytes 50332672 | tf_op jit(solution)/shard_map/scatter-add | solution.py:38
  202.8 1.7 slice.20
  204.5 3.4 %all-to-all-start.1 = ((f32[8,64,128]{2,1,0:T(8,128)}), f32[8,64,128]{2,1,0:T(8,128)S(1)}, u32[]{:S(2)}, u32[]{:S(2)}) async-start(f32[8,64,128]{2,1,0:T(8,128)} %bitcast.18), calls=%async_computation.1 | async-start | bytes 524288 | tf_op jit(solution)/shard_map/all_to_all | solution.py:42
  207.9 0.0 all-reduce.3.cloned.1.call-start
  208.0 0.0 copy-start.1
  208.0 4.7 %slice.19 = f32[64,128,128]{2,1,0:T(8,128)} slice(f32[68,128,128]{2,1,0:T(8,128)} %scatter_fusion.1), slice={[0:64], [0:128], [0:128]} | slice | bytes 8388608 | tf_op jit(solution)/shard_map/slice | solution.py:40
  212.6 1.0 fusion.2
  213.6 0.0 all-reduce.3.cloned.1.call-update
  213.6 0.0 reduce-scatter.2.cloned.1.call-start
  213.7 2.4 all-to-all-done.1
  216.0 0.1 broadcast_select_fusion
  216.2 7.1 %scatter_fusion.2 = f32[8192,128]{1,0:T(8,128)} fusion(f32[8192,128]{1,0:T(8,128)} %bitcast.41, s32[512]{0:T(512)S(1)} %bitcast.47, f32[512,128]{1,0:T(8,128)S(1)} %bitcast.44), kind=kCustom, calls=%fused_computation.5 | custom fusion | flops 65536 | bytes 788480 | tf_op jit(solution)/shard_map/scatter-add | solution.py:44
  223.3 0.0 reduce-scatter.2.cloned.1.call-update
  223.3 0.0 all-reduce.5.cloned.1.call-start
  223.4 62.2 %all-reduce.3.cloned.1.call-done = f32[128,256]{1,0:T(8,128)} async-done(((f32[128,256]{1,0:T(8,128)}), f32[128,256]{1,0:T(8,128)}) %all-reduce.3.cloned.1.call-update) | async-done | bytes 131088 | tf_op jit(solution)/shard_map/psum | solution.py:34
  285.6 0.0 all-reduce.5.cloned.1.call-update
  285.6 0.0 reduce-scatter.2.cloned.1.call-done
  285.6 2.1 convert_element_type.27
  287.7 28.7 %all-reduce.5.cloned.1.call-done = f32[128,256]{1,0:T(8,128)} async-done(((f32[128,256]{1,0:T(8,128)}), f32[128,256]{1,0:T(8,128)}) %all-reduce.5.cloned.1.call-update) | async-done | bytes 131088 | tf_op jit(solution)/shard_map/psum | solution.py:34
  316.4 1.6 copy.24
  317.9 0.0 copy-done.1
  (4 shorter events, 0.0 us)
Async XLA Ops:
  8.0 97.6 %copy-start = (bf16[128,256]{1,0:T(8,128)(2,1)S(1)}, bf16[128,256]{1,0:T(8,128)(2,1)}, u32[]{:S(2)}) copy-start(bf16[128,256]{1,0:T(8,128)(2,1)} %param.9) | copy-start | bytes 196612
  13.3 14.6 %all-to-all-start = ((bf16[8,64,128]{2,1,0:T(8,128)(2,1)}), bf16[8,64,128]{2,1,0:T(8,128)(2,1)S(1)}, u32[]{:S(2)}, u32[]{:S(2)}) async-start(bf16[8,64,128]{2,1,0:T(8,128)(2,1)} %broadcast_select_fusion.1), calls=%async_computation | async-start | bytes 262144 | tf_op jit(solution)/shard_map/all_to_all | solution.py:17
  54.7 17.6 %copy-start.2 = (s32[1,1,256]{2,1,0:T(1,128)S(1)}, s32[1,1,256]{2,1,0:T(1,128)}, u32[]{:S(2)}) copy-start(s32[1,1,256]{2,1,0:T(1,128)} %param.13) | copy-start | bytes 3076
  72.3 33.3 %copy-start.4 = (bf16[2048,256]{1,0:T(8,128)(2,1)S(1)}, bf16[2048,256]{1,0:T(8,128)(2,1)}, u32[]{:S(2)}) copy-start(bf16[2048,256]{1,0:T(8,128)(2,1)} %param.10) | copy-start | bytes 3145732
  131.2 20.1 %copy-start.3 = (s32[1,1,256]{2,1,0:T(1,128)S(1)}, s32[1,1,256]{2,1,0:T(1,128)}, u32[]{:S(2)}) copy-start(s32[1,1,256]{2,1,0:T(1,128)} %param.14) | copy-start | bytes 3076
  204.5 11.6 %all-to-all-start.1 = ((f32[8,64,128]{2,1,0:T(8,128)}), f32[8,64,128]{2,1,0:T(8,128)S(1)}, u32[]{:S(2)}, u32[]{:S(2)}) async-start(f32[8,64,128]{2,1,0:T(8,128)} %bitcast.18), calls=%async_computation.1 | async-start | bytes 524288 | tf_op jit(solution)/shard_map/all_to_all | solution.py:42
  207.9 77.7 %all-reduce.3.cloned.1.call-start = ((), (), s32[]{:S(2)}) async-start(), calls=%async_computation.4 | async-start | bytes 262144 | tf_op jit(solution)/shard_map/psum | solution.py:34
  208.0 110.0 %copy-start.1 = (bf16[128,256]{1,0:T(8,128)(2,1)S(1)}, bf16[128,256]{1,0:T(8,128)(2,1)}, u32[]{:S(2)}) copy-start(bf16[128,256]{1,0:T(8,128)(2,1)} %param.9) | copy-start | bytes 196612
  213.6 72.0 %reduce-scatter.2.cloned.1.call-start = ((), (), s32[]{:S(2)}) async-start(), calls=%async_computation.3 | async-start | bytes 5242880 | tf_op jit(solution)/shard_map/reduce_scatter | solution.py:45
  223.3 93.1 %all-reduce.5.cloned.1.call-start = ((), (), s32[]{:S(2)}) async-start(), calls=%async_computation.5 | async-start | bytes 262144 | tf_op jit(solution)/shard_map/psum | solution.py:34
Sparse Core Ops, SparseCore 0:
  213.8 71.7 all-reduce.2
Sparse Core Ops, SparseCore 1:
  223.4 43.4 reduce-scatter.1
  285.7 30.6 all-reduce.4
